TPU v7x, 768 devices: a whole 4x8x12 slice. The times are simulated.
768 devices in a mesh: space: 64 (over z_lo, y, core), filt: 12 (over z_hi, x).
Axes of the slice: x: 4, y: 8, z: 12 (z_hi: 3, z_lo: 4; z = z_hi * 4 + z_lo), core: 2. Of those that a mesh axis runs over, the one named last changes fastest.
Arguments:
- volumes: bfloat16 [2, 48, 256, 16, 4, 128], P(None, 'filt', 'space'), may hold values from -6 to 6
- first_kernel: bfloat16 [3, 3, 3, 32, 16], replicated, may hold values from -0.3125 to 0.3125
- deep_kernel: bfloat16 [3, 3, 3, 64, 32], replicated, may hold values from -0.21875 to 0.21875
Outputs:
- deep_out: bfloat16 [64, 2, 12, 64, 128], P('space', None, 'filt')
All inputs are finite; a program needn't handle non-finite values.
Results may differ from a plain program's by a relative error of at most 0.0048.
Values may be sent and summed in bfloat16 or wider, within the bound.
A program may use at most 32 MiB of HBM per device.

v0:
```python
import jax
import jax.numpy as jnp
from jax import lax
from jax.sharding import PartitionSpec as P


def passed_along(value, axis, steps):
    count = lax.axis_size(axis)
    leading, last = (max(0, -steps), min(count, count - steps))
    return lax.ppermute(value, axis, [(source, source + steps) for source in range(leading, last)])


def leaky(value):
    return jnp.where(value >= 0, value, 0.3 * value)


def shift_lane(field):
    return jnp.pad(field[..., :-1], ((0, 0), (0, 0), (0, 0), (0, 0), (1, 0)))


def strided_conv(fields, kernel, count_x, count_y, form):
    total = None
    for tap_a in range(3):
        for tap_b in range(3):
            for tap_c in range(3):
                source = fields[tap_c]
                shape = source.shape
                slab = lax.slice(
                    source,
                    (0, tap_a, tap_b, 0, 0),
                    (
                        shape[0],
                        tap_a + 2 * count_x - 1,
                        tap_b + 2 * count_y - 1,
                        shape[3],
                        shape[4],
                    ),
                    (1, 2, 2, 1, 1),
                )
                term = jnp.einsum(
                    form, kernel[tap_a, tap_b, tap_c], slab, preferred_element_type=jnp.float32
                )
                total = term if total is None else total + term
    return total


def deep_layer(padded, kernel, count_x, count_y):
    fields = [shift_lane(padded[:, :, :, :, 1]), padded[:, :, :, :, 0], padded[:, :, :, :, 1]]
    return leaky(strided_conv(fields, kernel, count_x, count_y, "oc,vxycz->ovxyz")).astype(
        jnp.bfloat16
    )


def per_device(volumes, first_kernel, deep_kernel):
    brick_x = volumes.shape[1]
    brick_y = volumes.shape[2]
    planes = passed_along(volumes[:, brick_x - 3 :], "filt", 1)
    extended = jnp.concatenate([planes, volumes], axis=1)
    row_rim = passed_along(extended[:, :, brick_y - 1 :], "space", 1)
    extended = jnp.concatenate([row_rim, extended], axis=2)
    phases = [extended[:, :, :, :, which] for which in range(4)]
    count_x = brick_x // 2 + 1
    count_y = brick_y // 2
    even = leaky(
        strided_conv(
            [shift_lane(phases[3]), phases[0], phases[1]],
            first_kernel,
            count_x,
            count_y,
            "oc,vxycz->vxyoz",
        )
    )
    odd = leaky(
        strided_conv(
            [phases[1], phases[2], phases[3]], first_kernel, count_x, count_y, "oc,vxycz->vxyoz"
        )
    )
    hidden = jnp.stack([even, odd], axis=4).astype(jnp.bfloat16)
    edge = passed_along(hidden[:, :, brick_y // 2 - 1 :], "space", 1)
    padded = jnp.concatenate([edge, hidden], axis=2)
    finished = deep_layer(padded, deep_kernel, brick_x // 4, brick_y // 4)
    return lax.all_to_all(finished, "space", split_axis=0, concat_axis=3, tiled=True)


def solution(mesh):
    in_specs = (P(None, "filt", "space", None, None, None), P(), P())
    out_specs = P("space", None, "filt", None, None)
    return jax.shard_map(
        per_device, mesh=mesh, in_specs=in_specs, out_specs=out_specs, check_vma=False
    )
```

profile of v0, /device:TPU:7, one launch (start us, length us, event | category | flops | bytes accessed | tf_op | source)
XLA Modules:
  0.0 101.3 jit_solution(7664243838045981766)
XLA Ops:
  0.0 1.0 slice-done
  1.1 10.7 %collective-permute-start = (bf16[2,3,4,16,4,128]{5,3,2,1,0,4:T(8,128)(2,1)S(1)}, bf16[2,3,4,16,4,128]{5,3,2,1,0,4:T(8,128)(2,1)S(1)}, u32[]{:S(2)}, u32[]{:S(2)}) collective-permute-start(bf16[2,3,4,16,4,128]{5,3,2,1,0,4:T(8,128)(2,1)S(1)} %copy.39), channel_id=1, source_target_pairs={{0,1},{1,2},{2,3},{3,4},{4,5},{5,6},{6,7},{7,8},{8,9},{9,10},{10,1... | collective-permute-start | bytes 1179656 | tf_op jit(solution)/shard_map/ppermute | solution.py:10
  11.8 7.9 %collective-permute-done = bf16[2,3,4,16,4,128]{5,3,2,1,0,4:T(8,128)(2,1)S(1)} collective-permute-done((bf16[2,3,4,16,4,128]{5,3,2,1,0,4:T(8,128)(2,1)S(1)}, bf16[2,3,4,16,4,128]{5,3,2,1,0,4:T(8,128)(2,1)S(1)}, u32[]{:S(2)}, u32[]{:S(2)}) %collective-permute-start) | collective-permute-done | bytes 393248 | tf_op jit(solution)/shard_map/ppermute | solution.py:10
  19.9 4.8 %collective-permute-start.1 = (bf16[2,7,1,16,4,128]{5,3,2,1,0,4:T(8,128)(2,1)S(1)}, bf16[2,7,1,16,4,128]{5,3,2,1,0,4:T(8,128)(2,1)S(1)}, u32[]{:S(2)}, u32[]{:S(2)}) collective-permute-start(bf16[2,7,1,16,4,128]{5,3,2,1,0,4:T(8,128)(2,1)S(1)} %slice.613), channel_id=1, source_target_pairs={{0,12},{12,24},{24,36},{36,48},{48,60},{60,72},{72,84},{84,96},{96... | collective-permute-start | bytes 688136 | tf_op jit(solution)/shard_map/ppermute | solution.py:10
  24.7 2.9 %collective-permute-done.1 = bf16[2,7,1,16,4,128]{5,3,2,1,0,4:T(8,128)(2,1)S(1)} collective-permute-done((bf16[2,7,1,16,4,128]{5,3,2,1,0,4:T(8,128)(2,1)S(1)}, bf16[2,7,1,16,4,128]{5,3,2,1,0,4:T(8,128)(2,1)S(1)}, u32[]{:S(2)}, u32[]{:S(2)}) %collective-permute-start.1) | collective-permute-done | bytes 229408 | tf_op jit(solution)/shard_map/ppermute | solution.py:10
  27.8 0.2 fusion.82
  28.0 0.2 convolution_bitcast_fusion.12
  28.2 0.2 convolution_bitcast_fusion.10
  28.5 0.2 convolution_bitcast_fusion.13
  28.7 0.2 convolution_bitcast_fusion.15
  28.9 0.2 convolution_bitcast_fusion.16
  29.1 0.2 convolution_bitcast_fusion.18
  29.6 0.2 convolution_bitcast_fusion.11
  30.3 0.2 fusion.100
  30.9 0.2 convolution_bitcast_fusion.8
  31.3 0.2 convolution_bitcast_fusion.3
  31.6 0.2 convolution_bitcast_fusion.6
  32.2 0.2 convolution_bitcast_fusion.1
  32.4 0.2 convolution_bitcast_fusion.4
  32.9 0.2 convolution_add_fusion.30
  33.3 0.2 convolution_add_fusion.28
  34.0 0.2 convolution_add_fusion.25
  34.7 0.2 convolution_add_fusion.22
  35.4 0.2 convolution_add_fusion.19
  36.1 0.2 convolution_add_fusion.16
  39.4 0.3 fusion.36
  39.8 0.3 fusion.34
  40.2 4.5 %collective-permute-start.2 = (bf16[2,3,1,32,2,128]{5,3,2,1,0,4:T(8,128)(2,1)S(1)}, bf16[2,3,1,32,2,128]{5,3,2,1,0,4:T(8,128)(2,1)S(1)}, u32[]{:S(2)}, u32[]{:S(2)}) collective-permute-start(bf16[2,3,1,32,2,128]{5,3,2,1,0,4:T(8,128)(2,1)S(1)} %pad_maximum_fusion.1), channel_id=1, source_target_pairs={{0,12},{12,24},{24,36},{36,48},{48,60},{60,72},{72,84},{84,96},{96... | collective-permute-start | bytes 294920 | tf_op jit(solution)/shard_map/ppermute | solution.py:10
  44.7 1.6 %collective-permute-done.2 = bf16[2,3,1,32,2,128]{5,3,2,1,0,4:T(8,128)(2,1)S(1)} collective-permute-done((bf16[2,3,1,32,2,128]{5,3,2,1,0,4:T(8,128)(2,1)S(1)}, bf16[2,3,1,32,2,128]{5,3,2,1,0,4:T(8,128)(2,1)S(1)}, u32[]{:S(2)}, u32[]{:S(2)}) %collective-permute-start.2) | collective-permute-done | bytes 98336 | tf_op jit(solution)/shard_map/ppermute | solution.py:10
  47.0 0.2 convolution_add_fusion.44
  52.1 48.6 %all_to_all.18 = bf16[64,2,1,1,128]{4,1,3,2,0:T(2,128)(2,1)S(1)} all-to-all(bf16[64,2,1,1,128]{4,1,3,2,0:T(2,128)(2,1)S(1)} %copy.9), channel_id=1, replica_groups=mesh['space'=64,'filt'=12] {'space'}, dimensions={0} | all-to-all | bytes 65536 | tf_op jit(solution)/shard_map/all_to_all | solution.py:82
  100.7 0.6 copy.10
  (74 shorter events, 12.7 us)
Async XLA Ops:
  0.0 1.0 slice-start
  1.0 18.7 %copy-start = (bf16[2,4,4,16,4,128]{5,4,3,2,1,0:T(4,128)(2,1)S(1)}, bf16[2,4,4,16,4,128]{5,4,3,2,1,0:T(4,128)(2,1)}, u32[]{:S(2)}) copy-start(bf16[2,4,4,16,4,128]{5,4,3,2,1,0:T(4,128)(2,1)} %param.3) | copy-start | bytes 1572868
  1.1 18.6 %collective-permute-start = (bf16[2,3,4,16,4,128]{5,3,2,1,0,4:T(8,128)(2,1)S(1)}, bf16[2,3,4,16,4,128]{5,3,2,1,0,4:T(8,128)(2,1)S(1)}, u32[]{:S(2)}, u32[]{:S(2)}) collective-permute-start(bf16[2,3,4,16,4,128]{5,3,2,1,0,4:T(8,128)(2,1)S(1)} %copy.39), channel_id=1, source_target_pairs={{0,1},{1,2},{2,3},{3,4},{4,5},{5,6},{6,7},{7,8},{8,9},{9,10},{10,1... | collective-permute-start | bytes 1179656 | tf_op jit(solution)/shard_map/ppermute | solution.py:10
  19.9 7.8 %copy-start.1 = (bf16[3,3,3,32,16]{3,4,2,1,0:T(8,128)(2,1)S(1)}, bf16[3,3,3,32,16]{3,4,2,1,0:T(8,128)(2,1)}, u32[]{:S(2)}) copy-start(bf16[3,3,3,32,16]{3,4,2,1,0:T(8,128)(2,1)} %param.4) | copy-start | bytes 82948
  19.9 7.7 %collective-permute-start.1 = (bf16[2,7,1,16,4,128]{5,3,2,1,0,4:T(8,128)(2,1)S(1)}, bf16[2,7,1,16,4,128]{5,3,2,1,0,4:T(8,128)(2,1)S(1)}, u32[]{:S(2)}, u32[]{:S(2)}) collective-permute-start(bf16[2,7,1,16,4,128]{5,3,2,1,0,4:T(8,128)(2,1)S(1)} %slice.613), channel_id=1, source_target_pairs={{0,12},{12,24},{24,36},{36,48},{48,60},{60,72},{72,84},{84,96},{96... | collective-permute-start | bytes 688136 | tf_op jit(solution)/shard_map/ppermute | solution.py:10
  40.1 6.2 %copy-start.2 = (bf16[3,3,3,64,32]{3,4,2,1,0:T(8,128)(2,1)S(1)}, bf16[3,3,3,64,32]{3,4,2,1,0:T(8,128)(2,1)}, u32[]{:S(2)}) copy-start(bf16[3,3,3,64,32]{3,4,2,1,0:T(8,128)(2,1)} %param.5) | copy-start | bytes 331780
  40.2 6.1 %collective-permute-start.2 = (bf16[2,3,1,32,2,128]{5,3,2,1,0,4:T(8,128)(2,1)S(1)}, bf16[2,3,1,32,2,128]{5,3,2,1,0,4:T(8,128)(2,1)S(1)}, u32[]{:S(2)}, u32[]{:S(2)}) collective-permute-start(bf16[2,3,1,32,2,128]{5,3,2,1,0,4:T(8,128)(2,1)S(1)} %pad_maximum_fusion.1), channel_id=1, source_target_pairs={{0,12},{12,24},{24,36},{36,48},{48,60},{60,72},{72,84},{84,96},{96... | collective-permute-start | bytes 294920 | tf_op jit(solution)/shard_map/ppermute | solution.py:10
where the time goes:
time: 102 us; the launch traced here: 101 us
  blocking collectives  48.6 us (48%)
  starting transfers between devices  20 us (20%)
  matrix products  17.6 us (17%)
  waiting for transfers between devices  12.5 us (12%)
  local copies, waits for them, and re-layouts  2 us (2%)
    all_to_all x1, blocking collectives, per_device(): lax.all_to_all(finished, 'space', split_axis=0, concat_axis=3, tiled=True)  48.6 us
    ppermute x3, starting transfers between devices, passed_along(): lax.ppermute(value, axis, [(source, source + steps) for source in range(l...  20 us
    dot_general x81, matrix products, strided_conv(): jnp.einsum(form, kernel[tap_a, tap_b, tap_c], slab, preferred_element_typ...  17.6 us
    ppermute x3, waiting for transfers between devices, passed_along(): lax.ppermute(value, axis, [(source, source + steps) for source in range(l...  12.5 us
  transfers between devices with their start and end apart: 3, of which 3 were waited for; matrix products, arithmetic and copies ran while one was open for 0% of the time, Pallas kernels for 0%

commit v1 on v0

v1 whole, which is shorter than its diff:
```python
import functools

import jax
import jax.numpy as jnp
from jax import lax
from jax.experimental import pallas as pl
from jax.experimental.pallas import tpu as pltpu
from jax.sharding import PartitionSpec as P

MESH = pl.DeviceIdType.MESH


def leaky(value):
    return jnp.where(value >= 0, value, 0.3 * value)


def first_weights(kernel):
    taps_x, taps_y, _, filters, channels = kernel.shape
    tap = [kernel[:, :, t] for t in range(3)]
    none = jnp.zeros_like(tap[0])
    rows = [
        jnp.stack([tap[1], tap[2], none, none], axis=-1),
        jnp.stack([none, tap[0], tap[1], tap[2]], axis=-1),
        jnp.stack([none, none, none, tap[0]], axis=-1),
    ]
    table = jnp.concatenate(rows, axis=2)
    table = table.reshape(taps_x, taps_y, 3 * filters, 4 * channels)
    return jnp.swapaxes(table, 1, 2).reshape(taps_x, 3 * filters, taps_y * 4 * channels)


def deep_weights(kernel):
    taps_x, taps_y, _, filters, channels = kernel.shape
    tap = [kernel[:, :, t] for t in range(3)]
    none = jnp.zeros_like(tap[0])
    table = jnp.concatenate(
        [jnp.concatenate([tap[1], tap[2]], axis=-1), jnp.concatenate([none, tap[0]], axis=-1)],
        axis=2,
    )
    return jnp.swapaxes(table, 1, 2).reshape(taps_x, 2 * filters, taps_y * 2 * channels)


def shift_lane(value, lanes):
    parts = []
    for start in range(0, value.shape[1], lanes):
        part = pltpu.roll(value[:, start : start + lanes], 1, 1)
        lane = lax.broadcasted_iota(jnp.int32, part.shape, 1)
        parts.append(jnp.where(lane == 0, 0.0, part))
    return jnp.concatenate(parts, axis=1)


def dot(left, right):
    return jnp.dot(left, right, preferred_element_type=jnp.float32)


def brick_kernel(
    count_space,
    count_filt,
    vol,
    first,
    deep,
    out,
    row,
    upper,
    lower,
    part_out,
    part_in,
    sum_out,
    sum_in,
    blocks_out,
    blocks_in,
    send_sem,
    recv_sem,
    block_send,
    block_recv,
):
    volumes, _, _, cells, lanes = vol.shape
    me = lax.axis_index("space")
    column = lax.axis_index("filt")
    has_left, has_right = column > 0, column < count_filt - 1
    has_down, has_up = me > 0, me < count_space - 1
    barrier = pltpu.get_barrier_semaphore()

    def greet(step, carry):
        peer = lax.rem(me + step, count_space)
        pl.semaphore_signal(barrier, inc=1, device_id={"space": peer}, device_id_type=MESH)
        return carry

    @pl.when(has_left)
    def _():
        pl.semaphore_signal(barrier, inc=1, device_id={"filt": column - 1}, device_id_type=MESH)

    @pl.when(has_right)
    def _():
        pl.semaphore_signal(barrier, inc=1, device_id={"filt": column + 1}, device_id_type=MESH)

    lax.fori_loop(1, count_space, greet, 0)

    def to_up(which, source, target):
        return pltpu.make_async_remote_copy(
            src_ref=source,
            dst_ref=target,
            send_sem=send_sem.at[which],
            recv_sem=recv_sem.at[which],
            device_id={"space": me + 1},
            device_id_type=MESH,
        )

    def to_right(which, source, target):
        return pltpu.make_async_remote_copy(
            src_ref=source,
            dst_ref=target,
            send_sem=send_sem.at[which],
            recv_sem=recv_sem.at[which],
            device_id={"filt": column + 1},
            device_id_type=MESH,
        )

    last = vol.shape[2] - 1
    row_copy = to_up(0, vol.at[:, :, last], row)
    upper_copy = to_up(1, upper.at[2], upper.at[0])
    lower_copy = to_up(2, lower.at[2], lower.at[0])
    part_copies = [to_right(3 + j, part_out.at[j], part_in.at[j]) for j in range(2)]
    sum_copy = to_right(5, sum_out, sum_in)

    @pl.when(jnp.logical_not(has_down))
    def _():
        row[...] = jnp.zeros_like(row)
        upper[0] = jnp.zeros(upper.shape[1:], upper.dtype)
        lower[0] = jnp.zeros(lower.shape[1:], lower.dtype)

    @pl.when(jnp.logical_not(has_left))
    def _():
        part_in[...] = jnp.zeros_like(part_in)
        sum_in[...] = jnp.zeros_like(sum_in)

    def slab(plane, j):
        sides = []
        for v in range(volumes):
            if j == 0:
                own = vol[v, plane, 0:2].reshape(2 * cells, lanes)
                sides.append(jnp.concatenate([row[v, plane], own], axis=0))
            else:
                sides.append(vol[v, plane, 1:4].reshape(3 * cells, lanes))
        return jnp.concatenate(sides, axis=1)

    def first_sum(value):
        third = value.shape[0] // 3
        even = value[:third] + shift_lane(value[2 * third :], lanes)
        return jnp.concatenate([even, value[third : 2 * third]], axis=0)

    def deep_sum(value):
        half = value.shape[0] // 2
        return value[:half] + shift_lane(value[half:], lanes)

    def first_layer(j):
        three = slab(3, j)
        part_out[j] = first_sum(dot(first[0], three)).astype(jnp.bfloat16)
        one = slab(1, j)
        whole = dot(first[2], three) + dot(first[1], slab(2, j)) + dot(first[0], one)
        upper[1 + j] = leaky(first_sum(whole)).astype(jnp.bfloat16)
        return first_sum(dot(first[1], slab(0, j)) + dot(first[2], one))

    rest_1 = first_layer(1)
    pl.semaphore_wait(
        barrier,
        count_space - 1 + has_left.astype(jnp.int32) + has_right.astype(jnp.int32),
    )

    @pl.when(has_up)
    def _():
        row_copy.start()
        upper_copy.start()

    @pl.when(has_right)
    def _():
        part_copies[1].start()

    @pl.when(has_down)
    def _():
        row_copy.wait_recv()

    rest_0 = first_layer(0)

    @pl.when(has_right)
    def _():
        part_copies[0].start()

    @pl.when(has_down)
    def _():
        upper_copy.wait_recv()

    high = upper[...].reshape(3 * upper.shape[1], upper.shape[2])
    sum_out[...] = deep_sum(dot(deep[0], high)).astype(jnp.bfloat16)

    @pl.when(has_right)
    def _():
        sum_copy.start()

    total = dot(deep[2], high)

    @pl.when(has_left)
    def _():
        part_copies[1].wait_recv()

    lower[2] = leaky(rest_1 + part_in[1].astype(jnp.float32)).astype(jnp.bfloat16)

    @pl.when(has_up)
    def _():
        lower_copy.start()

    @pl.when(has_left)
    def _():
        part_copies[0].wait_recv()

    lower[1] = leaky(rest_0 + part_in[0].astype(jnp.float32)).astype(jnp.bfloat16)

    @pl.when(has_down)
    def _():
        lower_copy.wait_recv()

    total = total + dot(deep[1], lower[...].reshape(3 * lower.shape[1], lower.shape[2]))
    total = deep_sum(total)

    @pl.when(has_left)
    def _():
        sum_copy.wait_recv()

    total = leaky(total + sum_in[...].astype(jnp.float32))
    for v in range(volumes):
        blocks_out[:, v, :] = total[:, v * lanes : (v + 1) * lanes]

    def block_copy(step):
        peer = lax.rem(me + step, count_space)
        return pltpu.make_async_remote_copy(
            src_ref=blocks_out.at[peer],
            dst_ref=blocks_in.at[me],
            send_sem=block_send.at[step],
            recv_sem=block_recv.at[step],
            device_id={"space": peer},
            device_id_type=MESH,
        )

    def block_start(step, carry):
        block_copy(step).start()
        return carry

    def block_wait(step, carry):
        block_copy(step).wait()
        return carry

    lax.fori_loop(1, count_space, block_start, 0)
    blocks_in[pl.ds(me, 1)] = blocks_out[pl.ds(me, 1)]

    @pl.when(has_up)
    def _():
        row_copy.wait_send()
        upper_copy.wait_send()
        lower_copy.wait_send()

    @pl.when(has_right)
    def _():
        part_copies[0].wait_send()
        part_copies[1].wait_send()
        sum_copy.wait_send()

    lax.fori_loop(1, count_space, block_wait, 0)
    for v in range(volumes):
        out[v] = blocks_in[:, v, :].astype(out.dtype)


def per_device(volumes, first_kernel, deep_kernel):
    count_space, count_filt = lax.axis_size("space"), lax.axis_size("filt")
    vols, size_x, size_y, channels, phases, lanes = volumes.shape
    cells = channels * phases
    filters = deep_kernel.shape[3]
    hidden = 2 * first_kernel.shape[3]
    wide = vols * lanes
    bf16, f32 = jnp.bfloat16, jnp.float32
    vmem = pl.BlockSpec(memory_space=pltpu.VMEM)
    out = pl.pallas_call(
        functools.partial(brick_kernel, count_space, count_filt),
        out_shape=jax.ShapeDtypeStruct((vols, count_space, lanes), bf16),
        in_specs=[vmem] * 3,
        out_specs=vmem,
        scratch_shapes=[
            pltpu.VMEM((vols, size_x, cells, lanes), bf16),
            pltpu.VMEM((3, hidden, wide), bf16),
            pltpu.VMEM((3, hidden, wide), bf16),
            pltpu.VMEM((2, hidden, wide), bf16),
            pltpu.VMEM((2, hidden, wide), bf16),
            pltpu.VMEM((filters, wide), bf16),
            pltpu.VMEM((filters, wide), bf16),
            pltpu.VMEM((filters, vols, lanes), f32),
            pltpu.VMEM((count_space, vols, lanes), f32),
            pltpu.SemaphoreType.DMA((6,)),
            pltpu.SemaphoreType.DMA((6,)),
            pltpu.SemaphoreType.DMA((count_space,)),
            pltpu.SemaphoreType.DMA((count_space,)),
        ],
        compiler_params=pltpu.CompilerParams(collective_id=0, has_side_effects=True),
        name="bricks",
    )(
        volumes.reshape(vols, size_x, size_y, cells, lanes),
        first_weights(first_kernel),
        deep_weights(deep_kernel),
    )
    return out.reshape(1, vols, 1, count_space, lanes)


def solution(mesh):
    in_specs = (P(None, "filt", "space", None, None, None), P(), P())
    out_specs = P("space", None, "filt", None, None)
    return jax.shard_map(
        per_device, mesh=mesh, in_specs=in_specs, out_specs=out_specs, check_vma=False
    )
```

time: 102 us -> 38.1 us (0.37)
  blocking collectives: 48.6 us -> 0 us
  Pallas kernels: 0 us -> 33.4 us
  starting transfers between devices: 20 us -> 0 us
  matrix products: 17.6 us -> 0 us
  waiting for transfers between devices: 12.5 us -> 0 us
  local copies, waits for them, and re-layouts: 2 us -> 4.03 us
    all_to_all x1 -> x0, blocking collectives: 48.6 us -> none  [per_device(): lax.all_to_all(finished, 'space', split_axis=0, concat_axis=3, tiled=True)]
    pallas_call x0 -> x1, Pallas kernels: none -> 33.4 us  [per_device(): pl.pallas_call(functools.partial(brick_kernel, count_space, count_filt),...]
    ppermute x3 -> x0, starting transfers between devices: 20 us -> none  [passed_along(): lax.ppermute(value, axis, [(source, source + steps) for source in range(l...]
    dot_general x81 -> x0, matrix products: 17.6 us -> none  [strided_conv(): jnp.einsum(form, kernel[tap_a, tap_b, tap_c], slab, preferred_element_typ...]
    ppermute x3 -> x0, waiting for transfers between devices: 12.5 us -> none  [passed_along(): lax.ppermute(value, axis, [(source, source + steps) for source in range(l...]
    reshape x0 -> x2, local copies, waits for them, and re-layouts: none -> 1.62 us  [the longest x1 0.81 us: deep_weights(): jnp.swapaxes(table, 1, 2)]
    unnamed x8 -> x3, local copies, waits for them, and re-layouts: 0.12 us -> 1.5 us
    slice x3 -> x0, local copies, waits for them, and re-layouts: 1.03 us -> none  [the longest x2 1 us: per_device(): planes = passed_along(volumes[:, brick_x - 3:], 'filt', 1)]
  transfers between devices with their start and end apart: 3 -> 0, of which waited for: 3 -> 0; matrix products, arithmetic and copies ran while one was open for 0% -> 0% of each run, Pallas kernels for 0% -> 0%
where the time goes in v1:
time: 38.1 us; the launch traced here: 37.7 us
  Pallas kernels  33.4 us (88%)
  local copies, waits for them, and re-layouts  4.03 us (11%)
    pallas_call x1, Pallas kernels, per_device(): pl.pallas_call(functools.partial(brick_kernel, count_space, count_filt),...  33.4 us
    unnamed x3, local copies, waits for them, and re-layouts  1.5 us
    another operation x1, local copies, waits for them, and re-layouts, first_weights(): jnp.stack([tap[1], tap[2], none, none], axis=-1)  0.81 us
    reshape x1, local copies, waits for them, and re-layouts, deep_weights(): jnp.swapaxes(table, 1, 2)  0.81 us
    reshape x1, local copies, waits for them, and re-layouts, first_weights(): jnp.swapaxes(table, 1, 2)  0.8 us

profile of v1, /device:TPU:7, one launch (start us, length us, event | category | flops | bytes accessed | tf_op | source)
XLA Modules:
  0.0 37.7 jit_solution(9774374765074935501)
XLA Ops:
  0.0 0.8 %slice_bitcast_fusion.5 = (bf16[3,3,32,16,1]{2,3,1,0,4:T(8,128)(2,1)S(1)}, bf16[3,3,32,16,1]{2,3,1,0,4:T(8,128)(2,1)S(1)}, bf16[3,3,32,16,1]{2,3,1,0,4:T(8,128)(2,1)S(1)}) fusion(bf16[3,3,3,32,16]{3,4,2,1,0:T(8,128)(2,1)} %param.4), kind=kLoop, calls=%fused_computation.9 | loop fusion | bytes 55296 | tf_op jit(solution)/shard_map/stack;squeeze | solution.py:22
  0.8 0.2 maximum_maximum_fusion
  1.0 0.1 copy.12
  1.1 0.0 copy-start
  1.1 0.8 %copy.16.first = bf16[3,96,192]{2,1,0:T(8,128)(2,1)} copy(bf16[3,96,192]{1,2,0:T(8,128)(2,1)S(1)} %bitcast.34) | data formatting | bytes 221184 | tf_op jit(solution)/shard_map/reshape | solution.py:28
  1.9 0.1 copy-done
  2.0 0.1 fusion.1
  2.1 0.8 %copy.17.deep = bf16[3,128,192]{2,1,0:T(8,128)(2,1)} copy(bf16[3,128,192]{1,2,0:T(8,128)(2,1)S(1)} %bitcast.35) | data formatting | bytes 294912 | tf_op jit(solution)/shard_map/reshape | solution.py:39
  2.9 33.4 %bricks.1 = bf16[2,64,128]{2,1,0:T(8,128)(2,1)} custom-call(bf16[2,4,4,64,128]{4,3,2,1,0:T(8,128)(2,1)} %bitcast.36, bf16[3,96,192]{2,1,0:T(8,128)(2,1)} %copy.16.first, bf16[3,128,192]{2,1,0:T(8,128)(2,1)} %copy.17.deep), custom_call_target="tpu_custom_call" | custom-call | tf_op jit(solution)/shard_map/bricks/pallas_call | solution.py:280
  36.3 1.4 %copy.25 = bf16[1,2,1,64,128]{4,3,2,1,0:T(8,128)(2,1)} copy(bf16[1,2,1,64,128]{4,3,2,1,0:T(8,128)(2,1)} %bitcast.37) | data formatting | bytes 65536
  (3 shorter events, 0.0 us)
Async XLA Ops:
  1.1 0.9 %copy-start = (bf16[3,3,3,64,32]{3,4,2,1,0:T(8,128)(2,1)S(1)}, bf16[3,3,3,64,32]{3,4,2,1,0:T(8,128)(2,1)}, u32[]{:S(2)}) copy-start(bf16[3,3,3,64,32]{3,4,2,1,0:T(8,128)(2,1)} %param.5) | copy-start | bytes 331780

commit v2 on v1

--- a/solution.py
+++ b/solution.py
@@ -8,35 +8,38 @@
 from jax.sharding import PartitionSpec as P
 
 MESH = pl.DeviceIdType.MESH
+CORES, ROWS = 2, 8
+CIN, C1 = 16, 32
 
 
 def leaky(value):
     return jnp.where(value >= 0, value, 0.3 * value)
 
 
-def first_weights(kernel):
-    taps_x, taps_y, _, filters, channels = kernel.shape
-    tap = [kernel[:, :, t] for t in range(3)]
-    none = jnp.zeros_like(tap[0])
-    rows = [
-        jnp.stack([tap[1], tap[2], none, none], axis=-1),
-        jnp.stack([none, tap[0], tap[1], tap[2]], axis=-1),
-        jnp.stack([none, none, none, tap[0]], axis=-1),
-    ]
-    table = jnp.concatenate(rows, axis=2)
-    table = table.reshape(taps_x, taps_y, 3 * filters, 4 * channels)
-    return jnp.swapaxes(table, 1, 2).reshape(taps_x, 3 * filters, taps_y * 4 * channels)
-
-
-def deep_weights(kernel):
-    taps_x, taps_y, _, filters, channels = kernel.shape
-    tap = [kernel[:, :, t] for t in range(3)]
-    none = jnp.zeros_like(tap[0])
-    table = jnp.concatenate(
-        [jnp.concatenate([tap[1], tap[2]], axis=-1), jnp.concatenate([none, tap[0]], axis=-1)],
-        axis=2,
-    )
-    return jnp.swapaxes(table, 1, 2).reshape(taps_x, 2 * filters, taps_y * 2 * channels)
+def placement(shape, period, group, phases):
+    row = lax.broadcasted_iota(jnp.int32, shape, 0)
+    column = lax.broadcasted_iota(jnp.int32, shape, 1)
+    tap, channel = row // period, row % period
+    role, rest = column // group, column % group
+    if phases > 2:
+        phase, own = rest % phases, rest // phases
+    else:
+        phase, own = rest // period, rest % period
+    hit = jnp.logical_and(own == channel, phase == tap + 2 * role - 1)
+    return jnp.where(hit, 1.0, 0.0).astype(jnp.bfloat16)
+
+
+def place(raw, table, place_by, group):
+    for a in range(3):
+        for b in range(3):
+            both = lax.dot_general(
+                raw[a, b], place_by, (((0,), (0,)), ((), ())), preferred_element_type=jnp.float32
+            ).astype(jnp.bfloat16)
+            filters = both.shape[0]
+            for role in range(both.shape[1] // group):
+                table[a, role * filters : (role + 1) * filters, b * group : (b + 1) * group] = both[
+                    :, role * group : (role + 1) * group
+                ]
 
 
 def shift_lane(value, lanes):
@@ -55,10 +58,15 @@
 def brick_kernel(
     count_space,
     count_filt,
+    vol_in,
+    first_in,
+    deep_in,
+    out,
     vol,
+    first_raw,
+    deep_raw,
     first,
     deep,
-    out,
     row,
     upper,
     lower,
@@ -72,6 +80,8 @@
     recv_sem,
     block_send,
     block_recv,
+    load_sem,
+    known,
 ):
     volumes, _, _, cells, lanes = vol.shape
     me = lax.axis_index("space")
@@ -79,11 +89,36 @@
     has_left, has_right = column > 0, column < count_filt - 1
     has_down, has_up = me > 0, me < count_space - 1
     barrier = pltpu.get_barrier_semaphore()
-
-    def greet(step, carry):
-        peer = lax.rem(me + step, count_space)
-        pl.semaphore_signal(barrier, inc=1, device_id={"space": peer}, device_id_type=MESH)
-        return carry
+    core, y, z = me % CORES, (me // CORES) % ROWS, me // (CORES * ROWS)
+    count_z = count_space // (CORES * ROWS)
+    z_below, z_above = z > 0, z < count_z - 1
+    partner = me + 1 - 2 * core
+    across = me + 2 * core - 1
+    has_across = jnp.logical_and(across >= 0, across < count_space)
+
+    def beside(step):
+        return z * (CORES * ROWS) + ((y + step + ROWS) % ROWS) * CORES + core
+
+    def tell(semaphore, peer):
+        pl.semaphore_signal(semaphore, inc=1, device_id={"space": peer}, device_id_type=MESH)
+
+    def tell_z(semaphore):
+        @pl.when(z_below)
+        def _():
+            tell(semaphore, me - CORES * ROWS)
+
+        @pl.when(z_above)
+        def _():
+            tell(semaphore, me + CORES * ROWS)
+
+    tell(barrier, partner)
+    tell(barrier, beside(1))
+    tell(barrier, beside(-1))
+    tell_z(barrier)
+
+    @pl.when(has_across)
+    def _():
+        tell(barrier, across)
 
     @pl.when(has_left)
     def _():
@@ -93,7 +128,19 @@
     def _():
         pl.semaphore_signal(barrier, inc=1, device_id={"filt": column + 1}, device_id_type=MESH)
 
-    lax.fori_loop(1, count_space, greet, 0)
+    loads = [
+        pltpu.make_async_copy(source, target, load_sem.at[which])
+        for which, (source, target) in enumerate(
+            [(first_in, first_raw), (vol_in, vol), (deep_in, deep_raw)]
+        )
+    ]
+    for load in loads:
+        load.start()
+
+    def one(flag):
+        return flag.astype(jnp.int32)
+
+    z_peers = one(z_below) + one(z_above)
 
     def to_up(which, source, target):
         return pltpu.make_async_remote_copy(
@@ -116,7 +163,7 @@
         )
 
     last = vol.shape[2] - 1
-    row_copy = to_up(0, vol.at[:, :, last], row)
+    row_copy = to_up(0, vol_in.at[:, :, last], row)
     upper_copy = to_up(1, upper.at[2], upper.at[0])
     lower_copy = to_up(2, lower.at[2], lower.at[0])
     part_copies = [to_right(3 + j, part_out.at[j], part_in.at[j]) for j in range(2)]
@@ -160,20 +207,34 @@
         upper[1 + j] = leaky(first_sum(whole)).astype(jnp.bfloat16)
         return first_sum(dot(first[1], slab(0, j)) + dot(first[2], one))
 
+    pl.semaphore_wait(barrier, 3 + z_peers + one(has_across) + one(has_left) + one(has_right))
+
+    @pl.when(has_up)
+    def _():
+        row_copy.start()
+
+    tell(known.at[0], beside(1))
+    tell(known.at[0], beside(-1))
+    loads[0].wait()
+    place(first_raw, first, placement((3 * CIN, 3 * 4 * CIN), CIN, 4 * CIN, 4), 4 * CIN)
+    pl.semaphore_wait(known.at[0], 2)
+    tell(known.at[1], beside(2))
+    tell(known.at[1], beside(-2))
+    loads[1].wait()
     rest_1 = first_layer(1)
-    pl.semaphore_wait(
-        barrier,
-        count_space - 1 + has_left.astype(jnp.int32) + has_right.astype(jnp.int32),
-    )
 
     @pl.when(has_up)
     def _():
-        row_copy.start()
         upper_copy.start()
 
     @pl.when(has_right)
     def _():
         part_copies[1].start()
+
+    loads[2].wait()
+    place(deep_raw, deep, placement((3 * C1, 4 * C1), C1, 2 * C1, 2), 2 * C1)
+    pl.semaphore_wait(known.at[1], 2)
+    tell_z(known.at[2])
 
     @pl.when(has_down)
     def _():
@@ -197,6 +258,8 @@
         sum_copy.start()
 
     total = dot(deep[2], high)
+    pl.semaphore_wait(known.at[2], z_peers)
+    tell(known.at[3], (z + count_z // 2) % count_z * (CORES * ROWS) + me % (CORES * ROWS))
 
     @pl.when(has_left)
     def _():
@@ -207,6 +270,9 @@
     @pl.when(has_up)
     def _():
         lower_copy.start()
+
+    pl.semaphore_wait(known.at[3], 1)
+    tell(known.at[4], partner)
 
     @pl.when(has_left)
     def _():
@@ -248,6 +314,7 @@
         block_copy(step).wait()
         return carry
 
+    pl.semaphore_wait(known.at[4], 1)
     lax.fori_loop(1, count_space, block_start, 0)
     blocks_in[pl.ds(me, 1)] = blocks_out[pl.ds(me, 1)]
 
@@ -280,9 +347,14 @@
     out = pl.pallas_call(
         functools.partial(brick_kernel, count_space, count_filt),
         out_shape=jax.ShapeDtypeStruct((vols, count_space, lanes), bf16),
-        in_specs=[vmem] * 3,
+        in_specs=[pl.BlockSpec(memory_space=pltpu.MemorySpace.HBM)] * 3,
         out_specs=vmem,
         scratch_shapes=[
+            pltpu.VMEM((vols, size_x, size_y, cells, lanes), bf16),
+            pltpu.VMEM((3, 3, 3 * channels, hidden // 2), bf16),
+            pltpu.VMEM((3, 3, 3 * hidden // 2, filters), bf16),
+            pltpu.VMEM((3, 3 * hidden // 2, 3 * cells), bf16),
+            pltpu.VMEM((3, 2 * filters, 3 * hidden), bf16),
             pltpu.VMEM((vols, size_x, cells, lanes), bf16),
             pltpu.VMEM((3, hidden, wide), bf16),
             pltpu.VMEM((3, hidden, wide), bf16),
@@ -296,13 +368,17 @@
             pltpu.SemaphoreType.DMA((6,)),
             pltpu.SemaphoreType.DMA((count_space,)),
             pltpu.SemaphoreType.DMA((count_space,)),
+            pltpu.SemaphoreType.DMA((3,)),
+            pltpu.SemaphoreType.REGULAR((5,)),
         ],
-        compiler_params=pltpu.CompilerParams(collective_id=0, has_side_effects=True),
+        compiler_params=pltpu.CompilerParams(
+            collective_id=0, has_side_effects=True
+        ),
         name="bricks",
     )(
         volumes.reshape(vols, size_x, size_y, cells, lanes),
-        first_weights(first_kernel),
-        deep_weights(deep_kernel),
+        jnp.swapaxes(first_kernel, 3, 4).reshape(3, 3, 3 * channels, hidden // 2),
+        jnp.swapaxes(deep_kernel, 3, 4).reshape(3, 3, 3 * hidden // 2, filters),
     )
     return out.reshape(1, vols, 1, count_space, lanes)
 

time: 38.1 us -> 36.1 us (0.948)
  the two profiles are of different devices: /device:TPU:7 before, /device:TPU:257 now
where the time goes in v2:
time: 36.1 us; the launch traced here: 35.9 us
  Pallas kernels  34.5 us (96%)
  local copies, waits for them, and re-layouts  1.38 us (4%)
    pallas_call x1, Pallas kernels, per_device(): pl.pallas_call(functools.partial(brick_kernel, count_space, count_filt),...  34.5 us
    unnamed x1, local copies, waits for them, and re-layouts  1.38 us

profile of v2, /device:TPU:257, one launch (start us, length us, event | category | flops | bytes accessed | tf_op | source)
XLA Modules:
  0.0 35.9 jit_solution(10817249537783898353)
XLA Ops:
  0.0 34.5 %bricks.1 = bf16[2,64,128]{2,1,0:T(8,128)(2,1)} custom-call(bf16[2,4,4,64,128]{4,3,2,1,0:T(8,128)(2,1)} %bitcast.10, bf16[3,3,48,32]{3,2,1,0:T(8,128)(2,1)} %bitcast.13, bf16[3,3,96,64]{3,2,1,0:T(8,128)(2,1)} %bitcast.11), custom_call_target="tpu_custom_call" | custom-call | tf_op jit(solution)/shard_map/bricks/pallas_call | solution.py:347
  34.5 1.4 %copy.6 = bf16[1,2,1,64,128]{4,3,2,1,0:T(8,128)(2,1)} copy(bf16[1,2,1,64,128]{4,3,2,1,0:T(8,128)(2,1)} %bitcast.12) | data formatting | bytes 65536

commit v3 on v2

--- a/solution.py
+++ b/solution.py
@@ -29,8 +29,8 @@
     return jnp.where(hit, 1.0, 0.0).astype(jnp.bfloat16)
 
 
-def place(raw, table, place_by, group):
-    for a in range(3):
+def place(raw, table, place_by, group, taps_x):
+    for a in taps_x:
         for b in range(3):
             both = lax.dot_general(
                 raw[a, b], place_by, (((0,), (0,)), ((), ())), preferred_element_type=jnp.float32
@@ -199,13 +199,17 @@
         half = value.shape[0] // 2
         return value[:half] + shift_lane(value[half:], lanes)
 
-    def first_layer(j):
+    def first_part(j):
         three = slab(3, j)
         part_out[j] = first_sum(dot(first[0], three)).astype(jnp.bfloat16)
-        one = slab(1, j)
-        whole = dot(first[2], three) + dot(first[1], slab(2, j)) + dot(first[0], one)
+        return three
+
+    def first_upper(j, three):
+        whole = dot(first[2], three) + dot(first[1], slab(2, j)) + dot(first[0], slab(1, j))
         upper[1 + j] = leaky(first_sum(whole)).astype(jnp.bfloat16)
-        return first_sum(dot(first[1], slab(0, j)) + dot(first[2], one))
+
+    def first_rest(j):
+        return first_sum(dot(first[1], slab(0, j)) + dot(first[2], slab(1, j)))
 
     pl.semaphore_wait(barrier, 3 + z_peers + one(has_across) + one(has_left) + one(has_right))
 
@@ -216,35 +220,41 @@
     tell(known.at[0], beside(1))
     tell(known.at[0], beside(-1))
     loads[0].wait()
-    place(first_raw, first, placement((3 * CIN, 3 * 4 * CIN), CIN, 4 * CIN, 4), 4 * CIN)
+    spots = placement((3 * CIN, 3 * 4 * CIN), CIN, 4 * CIN, 4)
+    place(first_raw, first, spots, 4 * CIN, (0,))
+    loads[1].wait()
+    three = first_part(1)
+
+    @pl.when(has_right)
+    def _():
+        part_copies[1].start()
+
     pl.semaphore_wait(known.at[0], 2)
     tell(known.at[1], beside(2))
     tell(known.at[1], beside(-2))
-    loads[1].wait()
-    rest_1 = first_layer(1)
+    place(first_raw, first, spots, 4 * CIN, (1, 2))
+    first_upper(1, three)
 
     @pl.when(has_up)
     def _():
         upper_copy.start()
 
+    @pl.when(has_down)
+    def _():
+        row_copy.wait_recv()
+
+    three = first_part(0)
+
     @pl.when(has_right)
     def _():
-        part_copies[1].start()
-
-    loads[2].wait()
-    place(deep_raw, deep, placement((3 * C1, 4 * C1), C1, 2 * C1, 2), 2 * C1)
+        part_copies[0].start()
+
     pl.semaphore_wait(known.at[1], 2)
     tell_z(known.at[2])
-
-    @pl.when(has_down)
-    def _():
-        row_copy.wait_recv()
-
-    rest_0 = first_layer(0)
-
-    @pl.when(has_right)
-    def _():
-        part_copies[0].start()
+    first_upper(0, three)
+    loads[2].wait()
+    spots = placement((3 * C1, 4 * C1), C1, 2 * C1, 2)
+    place(deep_raw, deep, spots, 2 * C1, (0,))
 
     @pl.when(has_down)
     def _():
@@ -257,6 +267,8 @@
     def _():
         sum_copy.start()
 
+    place(deep_raw, deep, spots, 2 * C1, (1, 2))
+    rest_1, rest_0 = first_rest(1), first_rest(0)
     total = dot(deep[2], high)
     pl.semaphore_wait(known.at[2], z_peers)
     tell(known.at[3], (z + count_z // 2) % count_z * (CORES * ROWS) + me % (CORES * ROWS))
@@ -292,30 +304,33 @@
         sum_copy.wait_recv()
 
     total = leaky(total + sum_in[...].astype(jnp.float32))
-    for v in range(volumes):
-        blocks_out[:, v, :] = total[:, v * lanes : (v + 1) * lanes]
-
-    def block_copy(step):
-        peer = lax.rem(me + step, count_space)
+    blocks_out[...] = jnp.stack(
+        [total[:, v * lanes : (v + 1) * lanes] for v in range(volumes)], axis=1
+    ).astype(jnp.bfloat16)
+
+    turn = jnp.where(z < count_z // 2, 1, -1)
+
+    def block_copy(source, target, peer):
         return pltpu.make_async_remote_copy(
-            src_ref=blocks_out.at[peer],
-            dst_ref=blocks_in.at[me],
-            send_sem=block_send.at[step],
-            recv_sem=block_recv.at[step],
+            src_ref=source,
+            dst_ref=target,
+            send_sem=block_send,
+            recv_sem=block_recv,
             device_id={"space": peer},
             device_id_type=MESH,
         )
 
-    def block_start(step, carry):
-        block_copy(step).start()
+    strides = next(n for n in (7, 3, 1) if (count_space - 1) % n == 0)
+
+    def block_starts(step, carry):
+        for k in range(strides):
+            away = turn * (count_space - 1 - step * strides - k)
+            peer = lax.rem(me + count_space + away, count_space)
+            block_copy(blocks_out.at[peer], blocks_in.at[me], peer).start()
         return carry
 
-    def block_wait(step, carry):
-        block_copy(step).wait()
-        return carry
-
     pl.semaphore_wait(known.at[4], 1)
-    lax.fori_loop(1, count_space, block_start, 0)
+    lax.fori_loop(0, (count_space - 1) // strides, block_starts, 0)
     blocks_in[pl.ds(me, 1)] = blocks_out[pl.ds(me, 1)]
 
     @pl.when(has_up)
@@ -330,9 +345,11 @@
         part_copies[1].wait_send()
         sum_copy.wait_send()
 
-    lax.fori_loop(1, count_space, block_wait, 0)
+    others = pl.ds(0, count_space - 1)
+    block_copy(blocks_out.at[others], blocks_in.at[others], partner).wait()
+    whole = blocks_in[...].astype(jnp.float32)
     for v in range(volumes):
-        out[v] = blocks_in[:, v, :].astype(out.dtype)
+        out[v] = whole[:, v, :].astype(out.dtype)
 
 
 def per_device(volumes, first_kernel, deep_kernel):
@@ -346,7 +363,7 @@
     vmem = pl.BlockSpec(memory_space=pltpu.VMEM)
     out = pl.pallas_call(
         functools.partial(brick_kernel, count_space, count_filt),
-        out_shape=jax.ShapeDtypeStruct((vols, count_space, lanes), bf16),
+        out_shape=pltpu.VMEM((vols, count_space, lanes), bf16),
         in_specs=[pl.BlockSpec(memory_space=pltpu.MemorySpace.HBM)] * 3,
         out_specs=vmem,
         scratch_shapes=[
@@ -362,12 +379,12 @@
             pltpu.VMEM((2, hidden, wide), bf16),
             pltpu.VMEM((filters, wide), bf16),
             pltpu.VMEM((filters, wide), bf16),
-            pltpu.VMEM((filters, vols, lanes), f32),
-            pltpu.VMEM((count_space, vols, lanes), f32),
+            pltpu.VMEM((filters, vols, lanes), bf16),
+            pltpu.VMEM((count_space, vols, lanes), bf16),
             pltpu.SemaphoreType.DMA((6,)),
             pltpu.SemaphoreType.DMA((6,)),
-            pltpu.SemaphoreType.DMA((count_space,)),
-            pltpu.SemaphoreType.DMA((count_space,)),
+            pltpu.SemaphoreType.DMA,
+            pltpu.SemaphoreType.DMA,
             pltpu.SemaphoreType.DMA((3,)),
             pltpu.SemaphoreType.REGULAR((5,)),
         ],

time: 36.1 us -> 30.7 us (0.85)
  the two profiles are of different devices: /device:TPU:257 before, /device:TPU:7 now
where the time goes in v3:
time: 30.7 us; the launch traced here: 30.2 us
  Pallas kernels  29.6 us (96%)
  local copies, waits for them, and re-layouts  0.62 us (2%)
    pallas_call x1, Pallas kernels, per_device(): pl.pallas_call(functools.partial(brick_kernel, count_space, count_filt),...  29.6 us
    unnamed x1, local copies, waits for them, and re-layouts  0.62 us

profile of v3, /device:TPU:7, one launch (start us, length us, event | category | flops | bytes accessed | tf_op | source)
XLA Modules:
  0.0 30.2 jit_solution(18231280037646682447)
XLA Ops:
  0.0 29.6 %bricks.1 = bf16[2,64,128]{2,1,0:T(8,128)(2,1)S(1)} custom-call(bf16[2,4,4,64,128]{4,3,2,1,0:T(8,128)(2,1)} %bitcast.11, bf16[3,3,48,32]{3,2,1,0:T(8,128)(2,1)} %bitcast.13, bf16[3,3,96,64]{3,2,1,0:T(8,128)(2,1)} %bitcast.12), custom_call_target="tpu_custom_call" | custom-call | tf_op jit(solution)/shard_map/bricks/pallas_call | solution.py:364
  29.6 0.6 %copy.6 = bf16[1,2,1,64,128]{4,3,2,1,0:T(8,128)(2,1)} copy(bf16[1,2,1,64,128]{4,3,2,1,0:T(8,128)(2,1)S(1)} %bitcast.10) | data formatting | bytes 65536

commit v4 on v3

--- a/solution.py
+++ b/solution.py
@@ -211,20 +211,20 @@
     def first_rest(j):
         return first_sum(dot(first[1], slab(0, j)) + dot(first[2], slab(1, j)))
 
-    pl.semaphore_wait(barrier, 3 + z_peers + one(has_across) + one(has_left) + one(has_right))
-
-    @pl.when(has_up)
-    def _():
-        row_copy.start()
-
-    tell(known.at[0], beside(1))
-    tell(known.at[0], beside(-1))
     loads[0].wait()
     spots = placement((3 * CIN, 3 * 4 * CIN), CIN, 4 * CIN, 4)
     place(first_raw, first, spots, 4 * CIN, (0,))
     loads[1].wait()
     three = first_part(1)
 
+    pl.semaphore_wait(barrier, 3 + z_peers + one(has_across) + one(has_left) + one(has_right))
+
+    @pl.when(has_up)
+    def _():
+        row_copy.start()
+
+    tell(known.at[0], beside(1))
+    tell(known.at[0], beside(-1))
     @pl.when(has_right)
     def _():
         part_copies[1].start()

time: 30.7 us -> 30.4 us (level)
  no operation moved by 1% of the time
where the time goes in v4:
time: 30.4 us; the launch traced here: 30.2 us
  Pallas kernels  29.6 us (97%)
  local copies, waits for them, and re-layouts  0.62 us (2%)
    pallas_call x1, Pallas kernels, per_device(): pl.pallas_call(functools.partial(brick_kernel, count_space, count_filt),...  29.6 us
    unnamed x1, local copies, waits for them, and re-layouts  0.62 us

profile of v4, /device:TPU:7, one launch (start us, length us, event | category | flops | bytes accessed | tf_op | source)
XLA Modules:
  0.0 30.2 jit_solution(516174011679059761)
XLA Ops:
  0.0 29.6 %bricks.1 = bf16[2,64,128]{2,1,0:T(8,128)(2,1)S(1)} custom-call(bf16[2,4,4,64,128]{4,3,2,1,0:T(8,128)(2,1)} %bitcast.11, bf16[3,3,48,32]{3,2,1,0:T(8,128)(2,1)} %bitcast.13, bf16[3,3,96,64]{3,2,1,0:T(8,128)(2,1)} %bitcast.12), custom_call_target="tpu_custom_call" | custom-call | tf_op jit(solution)/shard_map/bricks/pallas_call | solution.py:364
  29.6 0.6 %copy.6 = bf16[1,2,1,64,128]{4,3,2,1,0:T(8,128)(2,1)} copy(bf16[1,2,1,64,128]{4,3,2,1,0:T(8,128)(2,1)S(1)} %bitcast.10) | data formatting | bytes 65536
